TPU v7x, 128 devices: a whole 4x4x4 slice. The times are simulated.
128 devices in a mesh: row: 8 (over z, x_hi), col: 16 (over x_lo, y, core).
Axes of the slice: x: 4 (x_hi: 2, x_lo: 2; x = x_hi * 2 + x_lo), y: 4, z: 4, core: 2. Of those that a mesh axis runs over, the one named last changes fastest.
Arguments:
- eigvecs: bfloat16 [81920, 4096], P('row', 'col'), may hold values from -0.09375 to 0.09375
- reflectors: bfloat16 [2, 81920, 128], P(None, 'row'), may hold values from -6 to 6
- factors: float32 [2, 128, 128], replicated, may hold values from -0.00015258789 to 0.00015258789
- frequencies: float32 [4096], replicated, may hold values from 0.3 to 3
- region_blocks: int32 [72], P('row'), may hold values from 0 to 639, as said below
Outputs:
- covariance: float32 [9216, 9216], P('row', 'col')
Inputs may be any that keep to these rules, and one draw needn't show every extreme that they name: `region_blocks`: the 72 block numbers are distinct and ascending; exactly 9 of them lie in each consecutive run of 80 block numbers.
All inputs are finite; a program needn't handle non-finite values.
Results may differ from a plain program's by a relative error of at most 0.004.
Values may be sent and summed in bfloat16 or wider, within the bound.
No kernel may reach another device: no remote copies, remote signals or barrier semaphores. Data moves between devices by JAX's collectives and lax.ppermute only.
A program may use at most 128 MiB of HBM per device.

v0:
```python
import jax
import jax.numpy as jnp
from jax import lax
from jax.sharding import PartitionSpec as P

BLOCK = 128


def from_everyone(shard, axis):
    copies = jnp.broadcast_to(shard, (lax.axis_size(axis), *shard.shape))
    return lax.all_to_all(copies, axis, split_axis=0, concat_axis=0, tiled=True)


def over_copies(shard, axis):
    everything = from_everyone(shard, axis)
    return jnp.sum(everything, axis=0)


def contract_rows(left, right):
    return lax.dot_general(
        left, right, (((0,), (0,)), ((), ())), preferred_element_type=jnp.float32
    )


def contract_cols(left, right):
    return lax.dot_general(
        left, right, (((1,), (1,)), ((), ())), preferred_element_type=jnp.float32
    )


def per_device(eigvecs, reflectors, factors, frequencies, region_blocks):
    highest = lax.Precision.HIGHEST
    first_block = reflectors[0]
    second_block = reflectors[1]
    first_factor = jnp.triu(factors[0])
    second_factor = jnp.triu(factors[1])
    second_local = contract_rows(second_block, eigvecs)
    second_proj = over_copies(second_local, "row")
    second_apply = jnp.dot(second_factor, second_proj, precision=highest).astype(jnp.bfloat16)
    cross_local = contract_rows(first_block, second_block)
    first_local = contract_rows(first_block, eigvecs) - jnp.dot(
        cross_local, second_apply.astype(jnp.float32), precision=highest
    )
    first_proj = over_copies(first_local, "row")
    first_apply = jnp.dot(first_factor, first_proj, precision=highest).astype(jnp.bfloat16)
    local_blocks = eigvecs.shape[0] // BLOCK
    columns = eigvecs.shape[1]
    width = reflectors.shape[2]
    local_index = region_blocks - lax.axis_index("row") * local_blocks
    picked_vecs = jnp.take(
        eigvecs.reshape(local_blocks, BLOCK, columns), local_index, axis=0
    ).reshape(-1, columns)
    picked_refl = jnp.take(
        reflectors.reshape(2, local_blocks, BLOCK, width), local_index, axis=1
    ).reshape(2, -1, width)
    region = picked_vecs.astype(jnp.float32)
    region = region - jnp.dot(picked_refl[1], second_apply, preferred_element_type=jnp.float32)
    region = region - jnp.dot(picked_refl[0], first_apply, preferred_element_type=jnp.float32)
    region = region.astype(jnp.bfloat16)
    weight_all = 1.0 / jnp.tanh(frequencies / 2.0) / (2.0 * frequencies)
    column_index = lax.axis_index("col")
    weight = lax.dynamic_slice_in_dim(weight_all, column_index * columns, columns, 0)
    scaled = (region.astype(jnp.float32) * weight[None, :]).astype(jnp.bfloat16)
    whole = lax.all_gather(region, "row", axis=0, tiled=True)
    partner = lax.all_to_all(whole, "col", split_axis=0, concat_axis=1, tiled=True)
    return contract_cols(lax.all_gather(scaled, "col", axis=1, tiled=True), partner)


def solution(mesh):
    return jax.shard_map(
        per_device,
        mesh=mesh,
        in_specs=(P("row", "col"), P(None, "row", None), P(), P(), P("row")),
        out_specs=P("row", "col"),
        check_vma=False,
    )
```

profile of v0, /device:TPU:1, one launch (start us, length us, event | category | flops | bytes accessed | tf_op | source)
XLA Modules:
  0.0 266.3 jit_solution(2419679412700755586)
XLA Ops:
  6.5 0.0 copy-start.1
  6.5 4.3 %fusion.5 = f32[128,256]{1,0:T(8,128)S(1)} fusion(bf16[10240,256]{1,0:T(8,128)(2,1)} %param.5, bf16[2,10240,128]{2,1,0:T(8,128)(2,1)} %param.6), kind=kOutput, calls=%fused_computation.9 | convolution fusion | flops 671088640 | bytes 7995392 | tf_op jit(solution)/shard_map/dot_general | solution.py:20
  10.9 0.0 slice-start
  10.9 1.1 broadcast_in_dim.46
  11.9 8.3 %all-to-all-start = ((f32[8,128,256]{2,1,0:T(8,128)}), f32[8,128,256]{2,1,0:T(8,128)S(1)}, u32[]{:S(2)}, u32[]{:S(2)}) async-start(f32[8,128,256]{2,1,0:T(8,128)} %broadcast_in_dim.46), calls=%async_computation | async-start | bytes 2097152 | tf_op jit(solution)/shard_map/all_to_all | solution.py:11
  20.3 0.0 copy-done.1
  20.3 3.1 %gather_fusion.1 = bf16[9,2,128,128]{3,2,1,0:T(8,128)(2,1)S(1)} fusion(bf16[2,80,128,128]{3,2,1,0:T(8,128)(2,1)} %bitcast.46, s32[1024]{0:T(1024)S(1)} %pad_clamp_fusion), kind=kCustom, calls=%fused_computation.1 | custom fusion | bytes 1179684 | tf_op jit(solution)/shard_map/jit(_take)/gather | solution.py:53
  23.4 0.1 select_bitcast_fusion
  23.6 0.0 slice-start.1
  23.6 3.6 %fusion = f32[128,128]{1,0:T(8,128)S(1)} fusion(bf16[2,10240,128]{2,1,0:T(8,128)(2,1)} %param.6), kind=kOutput, calls=%fused_computation.4 | convolution fusion | flops 335544320 | bytes 5308416 | tf_op jit(solution)/shard_map/dot_general | solution.py:20
  27.2 0.0 slice-done
  27.2 0.1 slice-done.1
  27.3 0.0 copy-start
  27.3 2.8 %fusion.2 = f32[128,256]{1,0:T(8,128)S(1)} fusion(bf16[10240,256]{1,0:T(8,128)(2,1)S(1)} %bitcast.44, bf16[2,10240,128]{2,1,0:T(8,128)(2,1)} %param.6), kind=kOutput, calls=%fused_computation.6 | convolution fusion | flops 671088640 | bytes 7995392 | tf_op jit(solution)/shard_map/dot_general | solution.py:20
  30.2 6.1 %all-to-all-done = f32[8,128,256]{2,1,0:T(8,128)S(1)} async-done(((f32[8,128,256]{2,1,0:T(8,128)}), f32[8,128,256]{2,1,0:T(8,128)S(1)}, u32[]{:S(2)}, u32[]{:S(2)}) %all-to-all-start) | async-done | bytes 1048608 | tf_op jit(solution)/shard_map/all_to_all | solution.py:11
  36.2 0.1 reduce_sum.18
  36.3 0.0 copy-done
  36.3 0.3 convolution_convert_fusion.1
  36.6 0.2 convolution_subtract_fusion.2
  36.9 1.1 broadcast_in_dim.47
  37.9 4.1 %all-to-all-start.1 = ((f32[8,128,256]{2,1,0:T(8,128)}), f32[8,128,256]{2,1,0:T(8,128)S(1)}, u32[]{:S(2)}, u32[]{:S(2)}) async-start(f32[8,128,256]{2,1,0:T(8,128)} %broadcast_in_dim.47), calls=%async_computation.1 | async-start | bytes 2097152 | tf_op jit(solution)/shard_map/all_to_all | solution.py:11
  42.0 0.0 all-gather.5.cloned.1.call-start
  42.1 0.1 broadcast_bitcast_fusion
  42.2 3.1 %gather_fusion = bf16[9,128,256]{2,1,0:T(8,128)(2,1)S(1)} fusion(bf16[80,128,256]{2,1,0:T(8,128)(2,1)} %bitcast.42, s32[1024]{0:T(1024)S(1)} %pad_clamp_fusion), kind=kCustom, calls=%fused_computation | custom fusion | bytes 1179684 | tf_op jit(solution)/shard_map/jit(_take)/gather | solution.py:50
  45.2 0.8 multiply_divide_fusion
  46.0 0.2 bitcast_select_fusion
  46.2 0.3 convolution_subtract_fusion.1
  46.5 10.9 %all-to-all-done.1 = f32[8,128,256]{2,1,0:T(8,128)S(1)} async-done(((f32[8,128,256]{2,1,0:T(8,128)}), f32[8,128,256]{2,1,0:T(8,128)S(1)}, u32[]{:S(2)}, u32[]{:S(2)}) %all-to-all-start.1) | async-done | bytes 1048608 | tf_op jit(solution)/shard_map/all_to_all | solution.py:11
  57.4 0.1 reduce_sum.19
  57.5 0.3 convolution_convert_fusion
  57.8 1.3 multiply_convert_fusion
  59.1 0.0 all-gather.5.cloned.1.call-update
  59.2 0.0 all-gather.3.cloned.1.call-start
  59.2 0.7 all-gather.3.cloned.1.call-update
  59.9 74.4 %all-gather.5.cloned.1.call-done = bf16[9216,256]{1,0:T(8,128)(2,1)} async-done(((bf16[1152,256]{1,0:T(8,128)(2,1)}), bf16[9216,256]{1,0:T(8,128)(2,1)}) %all-gather.5.cloned.1.call-update) | async-done | bytes 4718608 | tf_op jit(solution)/shard_map/all_gather | solution.py:64
  134.3 77.2 %all_to_all.29 = bf16[16,576,256]{2,1,0:T(8,128)(2,1)S(1)} all-to-all(bf16[16,576,256]{2,1,0:T(8,128)(2,1)} %bitcast.47), channel_id=1, replica_groups=mesh['row'=8,'col'=16] {'col'}, dimensions={0} | all-to-all | bytes 9437184 | tf_op jit(solution)/shard_map/all_to_all | solution.py:65
  211.5 2.9 %copy.9 = bf16[16,72,8,256]{3,2,0,1:T(8,128)(2,1)} copy(bf16[16,72,8,256]{3,2,1,0:T(8,128)(2,1)S(1)} %bitcast.45) | data formatting | bytes 9437184 | tf_op jit(solution)/shard_map/all_to_all | solution.py:65
  214.4 33.2 %all-gather.3.cloned.1.call-done = bf16[1152,4096]{1,0:T(8,128)(2,1)} async-done(((bf16[1152,256]{1,0:T(8,128)(2,1)}), bf16[1152,4096]{1,0:T(8,128)(2,1)}) %all-gather.3.cloned.1.call-update) | async-done | bytes 9437200 | tf_op jit(solution)/shard_map/all_gather | solution.py:66
  247.5 12.0 %fusion.21 = f32[1152,576]{0,1:T(8,128)} fusion(bf16[1152,4096]{1,0:T(8,128)(2,1)} %all-gather.3.cloned.1.call-done, bf16[576,4096]{1,0:T(8,128)(2,1)} %bitcast.48), kind=kOutput, calls=%fused_computation.40 | convolution fusion | flops 5435817984 | bytes 16809984 | tf_op jit(solution)/shard_map/dot_general | solution.py:26
  (5 shorter events, 0.1 us)
Async XLA Ops:
  6.5 13.7 %copy-start.1 = (s32[9]{0:T(128)S(1)}, s32[9]{0:T(128)}, u32[]{:S(2)}) copy-start(s32[9]{0:T(128)} %param.9) | copy-start | bytes 112
  10.9 16.4 %slice-start = ((s8[5242880]{0:T(1024)(128)(4,1)}), s8[1048576]{0:T(1024)(128)(4,1)S(1)}, s32[]{:S(2)}) async-start(s8[5242880]{0:T(1024)(128)(4,1)} %bitcast.43), calls=%async_computation.5 | async-start | bytes 2097152
  11.9 24.3 %all-to-all-start = ((f32[8,128,256]{2,1,0:T(8,128)}), f32[8,128,256]{2,1,0:T(8,128)S(1)}, u32[]{:S(2)}, u32[]{:S(2)}) async-start(f32[8,128,256]{2,1,0:T(8,128)} %broadcast_in_dim.46), calls=%async_computation | async-start | bytes 2097152 | tf_op jit(solution)/shard_map/all_to_all | solution.py:11
  23.6 3.8 %slice-start.1 = ((s8[5242880]{0:T(1024)(128)(4,1)}), s8[4194304]{0:T(1024)(128)(4,1)S(1)}, s32[]{:S(2)}) async-start(s8[5242880]{0:T(1024)(128)(4,1)} %bitcast.43), calls=%async_computation.6 | async-start | bytes 8388608
  27.3 9.0 %copy-start = (f32[2,128,128]{2,1,0:T(8,128)S(1)}, f32[2,128,128]{2,1,0:T(8,128)}, u32[]{:S(2)}) copy-start(f32[2,128,128]{2,1,0:T(8,128)} %param.7) | copy-start | bytes 393220
  37.9 19.5 %all-to-all-start.1 = ((f32[8,128,256]{2,1,0:T(8,128)}), f32[8,128,256]{2,1,0:T(8,128)S(1)}, u32[]{:S(2)}, u32[]{:S(2)}) async-start(f32[8,128,256]{2,1,0:T(8,128)} %broadcast_in_dim.47), calls=%async_computation.1 | async-start | bytes 2097152 | tf_op jit(solution)/shard_map/all_to_all | solution.py:11
  42.0 92.3 %all-gather.5.cloned.1.call-start = ((), (), s32[]{:S(2)}) async-start(), calls=%async_computation.4 | async-start | bytes 5308416 | tf_op jit(solution)/shard_map/all_gather | solution.py:64
  59.2 188.4 %all-gather.3.cloned.1.call-start = ((), (), s32[]{:S(2)}) async-start(), calls=%async_computation.3 | async-start | bytes 10027008 | tf_op jit(solution)/shard_map/all_gather | solution.py:66
Sparse Core Ops, SparseCore 0:
  59.3 74.9 all-gather.4
  135.9 111.5 all-gather.2
where the time goes:
time: 267 us; the launch traced here: 266 us
  waiting for transfers between devices  125 us (47%)
  blocking collectives  77.2 us (29%)
  matrix products  25.1 us (9%)
  between operations  13.6 us (5%)
  starting transfers between devices  12.5 us (5%)
  local copies, waits for them, and re-layouts  11.4 us (4%)
    all_to_all x1, blocking collectives, per_device(): lax.all_to_all(whole, 'col', split_axis=0, concat_axis=1, tiled=True)  77.2 us
    all_gather x1, waiting for transfers between devices, per_device(): whole = lax.all_gather(region, 'row', axis=0, tiled=True)  74.4 us
    all_gather x1, waiting for transfers between devices, per_device(): lax.all_gather(scaled, 'col', axis=1, tiled=True)  33.2 us
    all_to_all x2, waiting for transfers between devices, from_everyone(): return lax.all_to_all(copies, axis, split_axis=0, concat_axis=0, tiled=True)  17 us
    all_to_all x2, starting transfers between devices, from_everyone(): return lax.all_to_all(copies, axis, split_axis=0, concat_axis=0, tiled=True)  12.4 us
    dot_general x1, matrix products, contract_cols(): lax.dot_general(left, right, (((1,), (1,)), ((), ())), preferred_element_...  12 us
    dot_general x3, matrix products, contract_rows(): lax.dot_general(left, right, (((0,), (0,)), ((), ())), preferred_element_...  10.7 us
  transfers between devices with their start and end apart: 4, of which 4 were waited for; matrix products, arithmetic and copies ran while one was open for 6% of the time, Pallas kernels for 0%

commit v1 on v0

--- a/solution.py
+++ b/solution.py
@@ -63,7 +63,12 @@
     scaled = (region.astype(jnp.float32) * weight[None, :]).astype(jnp.bfloat16)
     whole = lax.all_gather(region, "row", axis=0, tiled=True)
     partner = lax.all_to_all(whole, "col", split_axis=0, concat_axis=1, tiled=True)
-    return contract_cols(lax.all_gather(scaled, "col", axis=1, tiled=True), partner)
+    return contract_cols(
+        jnp.concatenate(
+            lax.all_to_all(jnp.stack(lax.psum(1, axis_name="col") * [scaled]), "col", 0, 0), axis=1
+        ),
+        partner,
+    )
 
 
 def solution(mesh):

time: 267 us -> 306 us (1.15)
  waiting for transfers between devices: 125 us -> 166 us
  blocking collectives: 77.2 us -> 68.4 us
  starting transfers between devices: 12.5 us -> 19.8 us
    all_to_all x0 -> x1, waiting for transfers between devices: none -> 40.7 us  [per_device(): lax.all_to_all(jnp.stack(lax.psum(1, axis_name='col') * [scaled]), 'col',...]
    all_gather x1, waiting for transfers between devices: 74.4 us -> 108 us  [per_device(): whole = lax.all_gather(region, 'row', axis=0, tiled=True)]
    all_gather x1 -> x0, waiting for transfers between devices: 33.2 us -> none  [per_device(): lax.all_gather(scaled, 'col', axis=1, tiled=True)]
    all_to_all x1, blocking collectives: 77.2 us -> 68.4 us  [per_device(): lax.all_to_all(whole, 'col', split_axis=0, concat_axis=1, tiled=True)]
    all_to_all x0 -> x1, starting transfers between devices: none -> 7.28 us  [per_device(): lax.all_to_all(jnp.stack(lax.psum(1, axis_name='col') * [scaled]), 'col',...]
    another operation x0 -> x1, local copies, waits for them, and re-layouts: none -> 4.56 us  [per_device(): jnp.stack(lax.psum(1, axis_name='col') * [scaled])]
  transfers between devices with their start and end apart: 4 -> 4, of which waited for: 4 -> 4; matrix products, arithmetic and copies ran while one was open for 6% -> 5% of each run, Pallas kernels for 0% -> 0%
where the time goes in v1:
time: 306 us
  waiting for transfers between devices  166 us (54%)
  blocking collectives  68.4 us (22%)
  matrix products  23.3 us (8%)
  starting transfers between devices  19.8 us (6%)
  between operations  13.6 us (4%)
  local copies, waits for them, and re-layouts  13.1 us (4%)
    all_gather x1, waiting for transfers between devices, per_device(): whole = lax.all_gather(region, 'row', axis=0, tiled=True)  108 us
    all_to_all x1, blocking collectives, per_device(): lax.all_to_all(whole, 'col', split_axis=0, concat_axis=1, tiled=True)  68.4 us
    all_to_all x1, waiting for transfers between devices, per_device(): lax.all_to_all(jnp.stack(lax.psum(1, axis_name='col') * [scaled]), 'col',...  40.7 us
    all_to_all x2, waiting for transfers between devices, from_everyone(): return lax.all_to_all(copies, axis, split_axis=0, concat_axis=0, tiled=True)  17 us
    all_to_all x2, starting transfers between devices, from_everyone(): return lax.all_to_all(copies, axis, split_axis=0, concat_axis=0, tiled=True)  12.4 us
    dot_general x3, matrix products, contract_rows(): lax.dot_general(left, right, (((0,), (0,)), ((), ())), preferred_element_...  10.7 us
    dot_general x1, matrix products, contract_cols(): lax.dot_general(left, right, (((1,), (1,)), ((), ())), preferred_element_...  10.4 us
    all_to_all x1, starting transfers between devices, per_device(): lax.all_to_all(jnp.stack(lax.psum(1, axis_name='col') * [scaled]), 'col',...  7.28 us
  transfers between devices with their start and end apart: 4, of which 4 were waited for; matrix products, arithmetic and copies ran while one was open for 5% of the time, Pallas kernels for 0%

profile of v1, /device:TPU:1, one launch (start us, length us, event | category | flops | bytes accessed | tf_op | source)
XLA Modules:
  0.0 305.8 jit_solution(5718852424751631668)
XLA Ops:
  6.5 0.0 copy-start.1
  6.5 4.3 %fusion.13 = f32[128,256]{1,0:T(8,128)S(1)} fusion(bf16[10240,256]{1,0:T(8,128)(2,1)} %param.5, bf16[2,10240,128]{2,1,0:T(8,128)(2,1)} %param.6), kind=kOutput, calls=%fused_computation.13 | convolution fusion | flops 671088640 | bytes 7995392 | tf_op jit(solution)/shard_map/dot_general | solution.py:20
  10.9 0.0 slice-start
  10.9 1.1 broadcast_in_dim.46
  11.9 8.3 %all-to-all-start = ((f32[8,128,256]{2,1,0:T(8,128)}), f32[8,128,256]{2,1,0:T(8,128)S(1)}, u32[]{:S(2)}, u32[]{:S(2)}) async-start(f32[8,128,256]{2,1,0:T(8,128)} %broadcast_in_dim.46), calls=%async_computation | async-start | bytes 2097152 | tf_op jit(solution)/shard_map/all_to_all | solution.py:11
  20.3 0.0 copy-done.1
  20.3 3.1 %gather_fusion.1 = bf16[9,2,128,128]{3,2,1,0:T(8,128)(2,1)S(1)} fusion(bf16[2,80,128,128]{3,2,1,0:T(8,128)(2,1)} %bitcast.52, s32[1024]{0:T(1024)S(1)} %pad_clamp_fusion), kind=kCustom, calls=%fused_computation.1 | custom fusion | bytes 1179684 | tf_op jit(solution)/shard_map/jit(_take)/gather | solution.py:53
  23.4 0.1 select_bitcast_fusion
  23.6 0.0 slice-start.1
  23.6 3.6 %fusion.8 = f32[128,128]{1,0:T(8,128)S(1)} fusion(bf16[2,10240,128]{2,1,0:T(8,128)(2,1)} %param.6), kind=kOutput, calls=%fused_computation.8 | convolution fusion | flops 335544320 | bytes 5308416 | tf_op jit(solution)/shard_map/dot_general | solution.py:20
  27.2 0.0 slice-done
  27.2 0.1 slice-done.1
  27.3 0.0 copy-start
  27.3 2.8 fusion.10
  30.2 6.1 %all-to-all-done = f32[8,128,256]{2,1,0:T(8,128)S(1)} async-done(((f32[8,128,256]{2,1,0:T(8,128)}), f32[8,128,256]{2,1,0:T(8,128)S(1)}, u32[]{:S(2)}, u32[]{:S(2)}) %all-to-all-start) | async-done | bytes 1048608 | tf_op jit(solution)/shard_map/all_to_all | solution.py:11
  36.2 0.1 reduce_sum.18
  36.3 0.0 copy-done
  36.3 0.3 convolution_convert_fusion.1
  36.6 0.2 convolution_subtract_fusion.2
  36.9 1.1 broadcast_in_dim.47
  37.9 4.1 %all-to-all-start.1 = ((f32[8,128,256]{2,1,0:T(8,128)}), f32[8,128,256]{2,1,0:T(8,128)S(1)}, u32[]{:S(2)}, u32[]{:S(2)}) async-start(f32[8,128,256]{2,1,0:T(8,128)} %broadcast_in_dim.47), calls=%async_computation.1 | async-start | bytes 2097152 | tf_op jit(solution)/shard_map/all_to_all | solution.py:11
  42.0 0.1 broadcast_bitcast_fusion
  42.1 3.1 %gather_fusion = bf16[9,128,256]{2,1,0:T(8,128)(2,1)S(1)} fusion(bf16[80,128,256]{2,1,0:T(8,128)(2,1)} %bitcast.49, s32[1024]{0:T(1024)S(1)} %pad_clamp_fusion), kind=kCustom, calls=%fused_computation | custom fusion | bytes 1179684 | tf_op jit(solution)/shard_map/jit(_take)/gather | solution.py:50
  45.2 0.8 multiply_divide_fusion
  46.0 0.2 bitcast_select_fusion
  46.2 0.3 convolution_subtract_fusion.1
  46.5 10.9 %all-to-all-done.1 = f32[8,128,256]{2,1,0:T(8,128)S(1)} async-done(((f32[8,128,256]{2,1,0:T(8,128)}), f32[8,128,256]{2,1,0:T(8,128)S(1)}, u32[]{:S(2)}, u32[]{:S(2)}) %all-to-all-start.1) | async-done | bytes 1048608 | tf_op jit(solution)/shard_map/all_to_all | solution.py:11
  57.4 0.1 reduce_sum.19
  57.5 0.3 convolution_convert_fusion
  57.8 1.1 multiply_convert_fusion
  59.0 4.6 %stack.2 = bf16[16,1152,256]{2,1,0:T(8,128)(2,1)} broadcast(bf16[1152,256]{1,0:T(8,128)(2,1)S(1)} %get-tuple-element.9), dimensions={1,2} | broadcast | bytes 10027008 | tf_op jit(solution)/shard_map/stack | solution.py:68
  63.5 7.3 %all-to-all-start.2 = ((bf16[16,1152,256]{2,1,0:T(8,128)(2,1)}), bf16[16,1152,256]{2,1,0:T(8,128)(2,1)}, u32[]{:S(2)}, u32[]{:S(2)}) async-start(bf16[16,1152,256]{2,1,0:T(8,128)(2,1)} %stack.2), calls=%async_computation.2 | async-start | bytes 18874368 | tf_op jit(solution)/shard_map/all_to_all | solution.py:68
  70.8 0.0 all-gather.2.cloned.1.call-start
  70.8 0.7 all-gather.2.cloned.1.call-update
  71.5 108.0 %all-gather.2.cloned.1.call-done = bf16[9216,256]{1,0:T(8,128)(2,1)} async-done(((bf16[1152,256]{1,0:T(8,128)(2,1)}), bf16[9216,256]{1,0:T(8,128)(2,1)}) %all-gather.2.cloned.1.call-update) | async-done | bytes 4718608 | tf_op jit(solution)/shard_map/all_gather | solution.py:64
  179.5 40.7 %all-to-all-done.2 = bf16[16,1152,256]{2,1,0:T(8,128)(2,1)} async-done(((bf16[16,1152,256]{2,1,0:T(8,128)(2,1)}), bf16[16,1152,256]{2,1,0:T(8,128)(2,1)}, u32[]{:S(2)}, u32[]{:S(2)}) %all-to-all-start.2) | async-done | bytes 9437216 | tf_op jit(solution)/shard_map/all_to_all | solution.py:68
  220.2 68.4 %all_to_all.31 = bf16[16,576,256]{2,1,0:T(8,128)(2,1)S(1)} all-to-all(bf16[16,576,256]{2,1,0:T(8,128)(2,1)} %bitcast.53), channel_id=1, replica_groups=mesh['row'=8,'col'=16] {'col'}, dimensions={0} | all-to-all | bytes 9437184 | tf_op jit(solution)/shard_map/all_to_all | solution.py:65
  288.5 10.4 %fusion.3 = f32[1152,576]{0,1:T(8,128)} fusion(bf16[16,576,256]{2,1,0:T(8,128)(2,1)S(1)} %all_to_all.31, bf16[16,1152,256]{2,1,0:T(8,128)(2,1)} %all-to-all-done.2), kind=kOutput, calls=%fused_computation.5 | convolution fusion | flops 5435817984 | bytes 16809984 | tf_op jit(solution)/shard_map/dot_general | solution.py:26
  (5 shorter events, 0.1 us)
Async XLA Ops:
  6.5 13.7 %copy-start.1 = (s32[9]{0:T(128)S(1)}, s32[9]{0:T(128)}, u32[]{:S(2)}) copy-start(s32[9]{0:T(128)} %param.9) | copy-start | bytes 112
  10.9 16.4 %slice-start = ((s8[5242880]{0:T(1024)(128)(4,1)}), s8[1048576]{0:T(1024)(128)(4,1)S(1)}, s32[]{:S(2)}) async-start(s8[5242880]{0:T(1024)(128)(4,1)} %bitcast.50), calls=%async_computation.5 | async-start | bytes 2097152
  11.9 24.3 %all-to-all-start = ((f32[8,128,256]{2,1,0:T(8,128)}), f32[8,128,256]{2,1,0:T(8,128)S(1)}, u32[]{:S(2)}, u32[]{:S(2)}) async-start(f32[8,128,256]{2,1,0:T(8,128)} %broadcast_in_dim.46), calls=%async_computation | async-start | bytes 2097152 | tf_op jit(solution)/shard_map/all_to_all | solution.py:11
  23.6 3.8 %slice-start.1 = ((s8[5242880]{0:T(1024)(128)(4,1)}), s8[4194304]{0:T(1024)(128)(4,1)S(1)}, s32[]{:S(2)}) async-start(s8[5242880]{0:T(1024)(128)(4,1)} %bitcast.50), calls=%async_computation.6 | async-start | bytes 8388608
  27.3 9.0 %copy-start = (f32[2,128,128]{2,1,0:T(8,128)S(1)}, f32[2,128,128]{2,1,0:T(8,128)}, u32[]{:S(2)}) copy-start(f32[2,128,128]{2,1,0:T(8,128)} %param.7) | copy-start | bytes 393220
  37.9 19.5 %all-to-all-start.1 = ((f32[8,128,256]{2,1,0:T(8,128)}), f32[8,128,256]{2,1,0:T(8,128)S(1)}, u32[]{:S(2)}, u32[]{:S(2)}) async-start(f32[8,128,256]{2,1,0:T(8,128)} %broadcast_in_dim.47), calls=%async_computation.1 | async-start | bytes 2097152 | tf_op jit(solution)/shard_map/all_to_all | solution.py:11
  63.5 156.6 %all-to-all-start.2 = ((bf16[16,1152,256]{2,1,0:T(8,128)(2,1)}), bf16[16,1152,256]{2,1,0:T(8,128)(2,1)}, u32[]{:S(2)}, u32[]{:S(2)}) async-start(bf16[16,1152,256]{2,1,0:T(8,128)(2,1)} %stack.2), calls=%async_computation.2 | async-start | bytes 18874368 | tf_op jit(solution)/shard_map/all_to_all | solution.py:68
  70.8 108.7 %all-gather.2.cloned.1.call-start = ((), (), s32[]{:S(2)}) async-start(), calls=%async_computation.4 | async-start | bytes 5308416 | tf_op jit(solution)/shard_map/all_gather | solution.py:64
Sparse Core Ops, SparseCore 0:
  73.9 105.5 all-gather.1
